TPU v7x, 32 devices: a whole 2x2x4 slice. The times are simulated.
32 devices in a mesh: grp: 2 (over core), dp: 4 (over y, x), sp: 4 (over z).
Axes of the slice: x: 2, y: 2, z: 4, core: 2. Of those that a mesh axis runs over, the one named last changes fastest.
Arguments:
- vis: bfloat16 [512, 5120], P(('grp', 'dp', 'sp')), may hold values from -6 to 6
- merge_weight: bfloat16 [5120, 8192], P('dp', ('grp', 'sp')), may hold values from -0.078125 to 0.078125
- img_counts: int32 [32], P('dp'), may hold values from 1 to 16
- img_pos: int32 [512], P(('grp', 'dp', 'sp')), may hold values from 0 to 127, as said below
- text: bfloat16 [4096, 8192], P(('grp', 'dp', 'sp')), may hold values from -6 to 6
- cot: bfloat16 [4096, 8192], P(('grp', 'dp', 'sp')), may hold values from -6 to 6
- gain: float32 [8192], replicated, may hold values from 0.25 to 1.75
Outputs:
- vis_grad: bfloat16 [512, 5120], P(('grp', 'dp', 'sp'))
- gain_grad: float32 [8192], replicated
Inputs may be any that keep to these rules, and one draw needn't show every extreme that they name: `img_pos`: within one device's block the 16 positions are distinct. `img_counts`: the counts of one image group sum to at most 128.
All inputs are finite; a program needn't handle non-finite values.
Results may differ from a plain program's by a relative error of at most 0.014.
Values may be sent and summed in bfloat16 or wider, within the bound.
No kernel may reach another device: no remote copies, remote signals or barrier semaphores. Data moves between devices by JAX's collectives and lax.ppermute only.
A program may use at most 128 MiB of HBM per device.

v0:
```python
import jax
import jax.numpy as jnp
from jax import lax
from jax.sharding import PartitionSpec as P


def body(vis, merge_weight, img_counts, img_pos, text, cot, gain):
    rows_dev = vis.shape[0]
    tok_rows = text.shape[0]
    group_vis = lax.all_gather(vis, ("grp", "sp"), axis=0, tiled=True)
    full_weight = lax.all_gather(merge_weight, "dp", axis=0, tiled=True)
    partial_value = jnp.dot(group_vis, full_weight, preferred_element_type=jnp.float32)
    emb = lax.all_to_all(
        partial_value.astype(jnp.bfloat16), ("grp", "sp"), split_axis=0, concat_axis=1, tiled=True
    )
    total_live = jnp.sum(img_counts)
    member = lax.axis_index("grp") * lax.axis_size("sp") + lax.axis_index("sp")
    group_row = member * rows_dev + jnp.arange(rows_dev, dtype=jnp.int32)
    live = group_row < total_live
    places = jnp.arange(tok_rows, dtype=jnp.int32)
    select = (img_pos[None, :] == places[:, None]) & live[None, :]
    taken = jnp.any(select, axis=1)
    select_b = select.astype(jnp.bfloat16)
    placed = jnp.dot(select_b, emb, preferred_element_type=jnp.float32)
    hidden = jnp.where(taken[:, None], placed, text.astype(jnp.float32))
    rinv = lax.rsqrt(jnp.mean(hidden * hidden, axis=1, keepdims=True) + 1e-06)
    cotf = cot.astype(jnp.float32)
    part_gain = jnp.sum(cotf * hidden * rinv, axis=0)
    scaled = cotf * gain[None, :]
    inner = jnp.mean(scaled * hidden, axis=1, keepdims=True)
    dhid = (rinv * scaled - hidden * rinv**3 * inner).astype(jnp.bfloat16)
    demb = jnp.dot(select_b.T, dhid, preferred_element_type=jnp.float32)
    demb = jnp.where(live[:, None], demb, 0.0).astype(jnp.bfloat16)
    returned = lax.all_to_all(demb, ("grp", "sp"), split_axis=1, concat_axis=0, tiled=True)
    terms = lax.dot_general(
        returned, full_weight, (((1,), (1,)), ((), ())), preferred_element_type=jnp.float32
    )
    vis_grad = lax.psum_scatter(
        terms.astype(jnp.bfloat16), ("grp", "sp"), scatter_dimension=0, tiled=True
    )
    gain_grad = lax.psum(part_gain, ("grp", "dp", "sp"))
    return (vis_grad, gain_grad)


def solution(mesh):
    return jax.shard_map(
        body,
        mesh=mesh,
        in_specs=(
            P(("grp", "dp", "sp"), None),
            P("dp", ("grp", "sp")),
            P("dp"),
            P(("grp", "dp", "sp")),
            P(("grp", "dp", "sp"), None),
            P(("grp", "dp", "sp"), None),
            P(),
        ),
        out_specs=(P(("grp", "dp", "sp"), None), P()),
        check_vma=False,
    )
```

profile of v0, /device:TPU:0, one launch (start us, length us, event | category | flops | bytes accessed | tf_op | source)
XLA Modules:
  0.0 229.6 jit_solution(17347707635758896386)
XLA Ops:
  7.2 0.0 all-gather.3.cloned.1.call-start
  7.2 0.7 all-gather.3.cloned.1.call-update
  7.9 0.0 all-gather.5.cloned.1.call-start
  7.9 0.7 all-gather.5.cloned.1.call-update
  8.7 27.1 %all-gather.3.cloned.1.call-done = bf16[128,5120]{1,0:T(8,128)(2,1)} async-done(((bf16[16,5120]{1,0:T(8,128)(2,1)}), bf16[128,5120]{1,0:T(8,128)(2,1)}) %all-gather.3.cloned.1.call-update) | async-done | bytes 1310736 | tf_op jit(solution)/shard_map/all_gather | solution.py:10
  35.7 106.3 %all-gather.5.cloned.1.call-done = bf16[5120,1024]{1,0:T(8,128)(2,1)} async-done(((bf16[1280,1024]{1,0:T(8,128)(2,1)}), bf16[5120,1024]{1,0:T(8,128)(2,1)}) %all-gather.5.cloned.1.call-update) | async-done | bytes 10485776 | tf_op jit(solution)/shard_map/all_gather | solution.py:11
  142.1 6.6 %convolution_convert_fusion.1 = bf16[128,1024]{1,0:T(8,128)(2,1)} fusion(bf16[128,5120]{1,0:T(8,128)(2,1)} %all-gather.3.cloned.1.call-done, bf16[5120,1024]{1,0:T(8,128)(2,1)} %all-gather.5.cloned.1.call-done), kind=kOutput, calls=%fused_computation.14 | convolution fusion | flops 1342308352 | bytes 12058624 | tf_op jit(solution)/shard_map/dot_general | solution.py:12
  148.7 4.7 %all-to-all-start = ((bf16[8,16,1024]{2,1,0:T(8,128)(2,1)}), bf16[8,16,1024]{2,1,0:T(8,128)(2,1)S(1)}, u32[]{:S(2)}, u32[]{:S(2)}) async-start(bf16[8,16,1024]{2,1,0:T(8,128)(2,1)} %bitcast), calls=%async_computation | async-start | bytes 524288 | tf_op jit(solution)/shard_map/all_to_all | solution.py:13
  153.4 0.0 reduce-scatter.2.cloned.1.call-start
  153.5 0.6 reduce_sum.36
  154.1 0.7 add_compare_fusion
  154.8 0.0 copy-done.3
  154.8 0.1 fusion.12
  154.9 7.9 %all-to-all-done = bf16[8,16,1024]{2,1,0:T(8,128)(2,1)S(1)} async-done(((bf16[8,16,1024]{2,1,0:T(8,128)(2,1)}), bf16[8,16,1024]{2,1,0:T(8,128)(2,1)S(1)}, u32[]{:S(2)}, u32[]{:S(2)}) %all-to-all-start) | async-done | bytes 262176 | tf_op jit(solution)/shard_map/all_to_all | solution.py:13
  162.8 0.0 slice-start
  162.8 1.0 multiply_reduce_fusion
  163.8 0.6 copy-done.1
  164.4 1.5 fusion.7
  165.9 1.1 fusion
  167.1 11.8 %all_to_all.38 = bf16[16,8,1024]{2,0,1:T(8,128)(2,1)S(1)} all-to-all(bf16[16,8,1024]{2,0,1:T(8,128)(2,1)S(1)} %bitcast.21), channel_id=1, replica_groups=mesh['grp'=2,'dp'=4,'sp'=4] {'grp','sp'}, dimensions={1} | all-to-all | bytes 524288 | tf_op jit(solution)/shard_map/all_to_all | solution.py:34
  178.9 0.0 slice-done.1
  178.9 4.6 %convolution_convert_fusion = bf16[128,5120]{1,0:T(8,128)(2,1)} fusion(bf16[128,1024]{1,0:T(8,128)(2,1)S(1)} %bitcast.19, bf16[5120,1024]{1,0:T(8,128)(2,1)S(1)} %bitcast.17), kind=kOutput, calls=%fused_computation.3 | convolution fusion | flops 1342832640 | bytes 12058624 | tf_op jit(solution)/shard_map/dot_general | solution.py:35
  183.5 0.0 reduce-scatter.2.cloned.1.call-update
  183.5 39.5 %psum.7 = f32[8192]{0:T(1024)} all-reduce(f32[8192]{0:T(1024)S(1)} %get-tuple-element.2), channel_id=1, replica_groups=mesh['grp'=2,'dp'=4,'sp'=4] {'grp','dp','sp'}, use_global_device_ids=true, to_apply=%region_6.7 | all-reduce | flops 8192 | bytes 65536 | tf_op jit(solution)/shard_map/psum | solution.py:41
  (18 shorter events, 0.1 us)
Async XLA Ops:
  7.2 28.6 %all-gather.3.cloned.1.call-start = ((), (), s32[]{:S(2)}) async-start(), calls=%async_computation.3 | async-start | bytes 1474560 | tf_op jit(solution)/shard_map/all_gather | solution.py:10
  7.9 134.2 %all-gather.5.cloned.1.call-start = ((), (), s32[]{:S(2)}) async-start(), calls=%async_computation.4 | async-start | bytes 13107200 | tf_op jit(solution)/shard_map/all_gather | solution.py:11
  8.6 144.8 %copy-start.4 = (s32[8]{0:T(128)S(1)}, s32[8]{0:T(128)}, u32[]{:S(2)}) copy-start(s32[8]{0:T(128)} %param.9) | copy-start | bytes 100
  8.7 146.1 %copy-start.3 = (s32[16]{0:T(128)S(1)}, s32[16]{0:T(128)}, u32[]{:S(2)}) copy-start(s32[16]{0:T(128)} %param.10) | copy-start | bytes 196
  8.7 154.1 %copy-start = (bf16[128,8192]{1,0:T(8,128)(2,1)S(1)}, bf16[128,8192]{1,0:T(8,128)(2,1)}, u32[]{:S(2)}) copy-start(bf16[128,8192]{1,0:T(8,128)(2,1)} %param.11) | copy-start | bytes 6291460
  148.7 15.1 %copy-start.2 = (f32[8192]{0:T(1024)S(1)}, f32[8192]{0:T(1024)}, u32[]{:S(2)}) copy-start(f32[8192]{0:T(1024)} %param.13) | copy-start | bytes 98308
  148.7 14.1 %all-to-all-start = ((bf16[8,16,1024]{2,1,0:T(8,128)(2,1)}), bf16[8,16,1024]{2,1,0:T(8,128)(2,1)S(1)}, u32[]{:S(2)}, u32[]{:S(2)}) async-start(bf16[8,16,1024]{2,1,0:T(8,128)(2,1)} %bitcast), calls=%async_computation | async-start | bytes 524288 | tf_op jit(solution)/shard_map/all_to_all | solution.py:13
  153.4 69.6 %reduce-scatter.2.cloned.1.call-start = ((), (), s32[]{:S(2)}) async-start(), calls=%async_computation.5 | async-start | bytes 1474560 | tf_op jit(solution)/shard_map/reduce_scatter | solution.py:38
  162.8 1.6 copy-start.1
  162.8 16.0 %slice-start = ((s8[10485760]{0:T(1024)(128)(4,1)}), s8[4194304]{0:T(1024)(128)(4,1)S(1)}, s32[]{:S(2)}) async-start(s8[10485760]{0:T(1024)(128)(4,1)} %bitcast.16), calls=%async_computation.6 | async-start | bytes 8388608
  164.4 14.5 %slice-start.1 = ((s8[10485760]{0:T(1024)(128)(4,1)}), s8[4194304]{0:T(1024)(128)(4,1)S(1)}, s32[]{:S(2)}) async-start(s8[10485760]{0:T(1024)(128)(4,1)} %bitcast.16), calls=%async_computation.7 | async-start | bytes 8388608
  165.9 13.0 %slice-start.2 = ((s8[10485760]{0:T(1024)(128)(4,1)}), s8[2097152]{0:T(1024)(128)(4,1)S(1)}, s32[]{:S(2)}) async-start(s8[10485760]{0:T(1024)(128)(4,1)} %bitcast.16), calls=%async_computation.8 | async-start | bytes 4194304
Sparse Core Ops, SparseCore 0:
  9.6 26.1 all-gather.2
  37.6 104.4 all-gather.4
  183.6 34.8 reduce-scatter.1
where the time goes:
time: 230 us
  waiting for transfers between devices  143 us (62%)
  blocking collectives  51.3 us (22%)
  between operations  13.9 us (6%)
  matrix products  13.4 us (6%)
  starting transfers between devices  4.85 us (2%)
  other arithmetic  2.91 us (1%)
    all_gather x1, waiting for transfers between devices, body(): full_weight = lax.all_gather(merge_weight, 'dp', axis=0, tiled=True)  106 us
    psum x1, blocking collectives, body(): gain_grad = lax.psum(part_gain, ('grp', 'dp', 'sp'))  39.5 us
    all_gather x1, waiting for transfers between devices, body(): group_vis = lax.all_gather(vis, ('grp', 'sp'), axis=0, tiled=True)  27.1 us
    all_to_all x1, blocking collectives, body(): lax.all_to_all(demb, ('grp', 'sp'), split_axis=1, concat_axis=0, tiled=True)  11.8 us
    all_to_all x1, waiting for transfers between devices, body(): lax.all_to_all(partial_value.astype(jnp.bfloat16), ('grp', 'sp'), split_a...  7.9 us
    dot_general x1, matrix products, body(): jnp.dot(group_vis, full_weight, preferred_element_type=jnp.float32)  6.62 us
    all_to_all x1, starting transfers between devices, body(): lax.all_to_all(partial_value.astype(jnp.bfloat16), ('grp', 'sp'), split_a...  4.74 us
    dot_general x1, matrix products, body(): lax.dot_general(returned, full_weight, (((1,), (1,)), ((), ())), preferre...  4.62 us
  transfers between devices with their start and end apart: 4, of which 3 were waited for; matrix products, arithmetic and copies ran while one was open for 1% of the time, Pallas kernels for 0%

commit v1 on v0

--- a/solution.py
+++ b/solution.py
@@ -1,13 +1,31 @@
+import functools
 import jax
 import jax.numpy as jnp
 from jax import lax
 from jax.sharding import PartitionSpec as P
 
 
+def fill_joints(local_values, ax_name):
+    low, left_arr = (lax.axis_size(ax_name), lax.axis_index(ax_name))
+    taken_in, everything = (local_values, 1)
+    while everything < low:
+        all_values = lax.ppermute(
+            taken_in, axis_name=ax_name, perm=list(map(lambda s: (s, s ^ everything), range(low)))
+        )
+        base_arr = jnp.concatenate([taken_in, all_values], axis=0)
+        all_rows = jnp.concatenate([all_values, taken_in], 0)
+        taken_in = jnp.where(left_arr & everything == 0, base_arr, all_rows)
+        everything = 2 * everything
+    return taken_in
+
+
+clear_ticks = functools.partial(fill_joints, ax_name=("grp", "sp"))
+
+
 def body(vis, merge_weight, img_counts, img_pos, text, cot, gain):
     rows_dev = vis.shape[0]
     tok_rows = text.shape[0]
-    group_vis = lax.all_gather(vis, ("grp", "sp"), axis=0, tiled=True)
+    group_vis = clear_ticks(vis)
     full_weight = lax.all_gather(merge_weight, "dp", axis=0, tiled=True)
     partial_value = jnp.dot(group_vis, full_weight, preferred_element_type=jnp.float32)
     emb = lax.all_to_all(

time: 230 us -> 205 us (0.89)
  waiting for transfers between devices: 143 us -> 111 us
  starting transfers between devices: 4.85 us -> 10.8 us
    all_gather x1 -> x0, waiting for transfers between devices: 27.1 us -> none  [body(): group_vis = lax.all_gather(vis, ('grp', 'sp'), axis=0, tiled=True)]
    all_gather x1, waiting for transfers between devices: 106 us -> 81.9 us  [body(): full_weight = lax.all_gather(merge_weight, 'dp', axis=0, tiled=True)]
    ppermute x0 -> x3, waiting for transfers between devices: none -> 20.5 us  [fill_joints(): lax.ppermute(taken_in, axis_name=ax_name, perm=list(map(lambda s: (s, s ^...]
    ppermute x0 -> x3, starting transfers between devices: none -> 6.01 us  [fill_joints(): lax.ppermute(taken_in, axis_name=ax_name, perm=list(map(lambda s: (s, s ^...]
  transfers between devices with their start and end apart: 4 -> 6, of which waited for: 3 -> 5; matrix products, arithmetic and copies ran while one was open for 1% -> 1% of each run, Pallas kernels for 0% -> 0%
where the time goes in v1:
time: 205 us
  waiting for transfers between devices  111 us (54%)
  blocking collectives  51.3 us (25%)
  between operations  14.2 us (7%)
  matrix products  13 us (6%)
  starting transfers between devices  10.8 us (5%)
  other arithmetic  4.08 us (2%)
    all_gather x1, waiting for transfers between devices, body(): full_weight = lax.all_gather(merge_weight, 'dp', axis=0, tiled=True)  81.9 us
    psum x1, blocking collectives, body(): gain_grad = lax.psum(part_gain, ('grp', 'dp', 'sp'))  39.6 us
    ppermute x3, waiting for transfers between devices, fill_joints(): lax.ppermute(taken_in, axis_name=ax_name, perm=list(map(lambda s: (s, s ^...  20.5 us
    all_to_all x1, blocking collectives, body(): lax.all_to_all(demb, ('grp', 'sp'), split_axis=1, concat_axis=0, tiled=True)  11.8 us
    all_to_all x1, waiting for transfers between devices, body(): lax.all_to_all(partial_value.astype(jnp.bfloat16), ('grp', 'sp'), split_a...  7.91 us
    dot_general x1, matrix products, body(): jnp.dot(group_vis, full_weight, preferred_element_type=jnp.float32)  6.23 us
    ppermute x3, starting transfers between devices, fill_joints(): lax.ppermute(taken_in, axis_name=ax_name, perm=list(map(lambda s: (s, s ^...  6.01 us
    all_to_all x1, starting transfers between devices, body(): lax.all_to_all(partial_value.astype(jnp.bfloat16), ('grp', 'sp'), split_a...  4.73 us
  transfers between devices with their start and end apart: 6, of which 5 were waited for; matrix products, arithmetic and copies ran while one was open for 1% of the time, Pallas kernels for 0%

profile of v1, /device:TPU:0, one launch (start us, length us, event | category | flops | bytes accessed | tf_op | source)
XLA Modules:
  0.0 205.0 jit_solution(11279214499522345765)
XLA Ops:
  7.2 0.0 all-gather.2.cloned.1.call-start
  7.2 0.7 all-gather.2.cloned.1.call-update
  7.9 3.1 %collective-permute-start = (bf16[16,5120]{1,0:T(8,128)(2,1)}, bf16[16,5120]{1,0:T(8,128)(2,1)S(1)}, u32[]{:S(2)}, u32[]{:S(2)}) collective-permute-start(bf16[16,5120]{1,0:T(8,128)(2,1)} %param.7), channel_id=1, source_target_pairs={{0,1},{1,0},{2,3},{3,2},{16,17},{17,16},{18,19},{19,18},{4,5},{5,4... | collective-permute-start | bytes 491528 | tf_op jit(solution)/shard_map/ppermute | solution.py:12
  11.0 4.4 %collective-permute-done = bf16[16,5120]{1,0:T(8,128)(2,1)S(1)} collective-permute-done((bf16[16,5120]{1,0:T(8,128)(2,1)}, bf16[16,5120]{1,0:T(8,128)(2,1)S(1)}, u32[]{:S(2)}, u32[]{:S(2)}) %collective-permute-start) | collective-permute-done | bytes 163872 | tf_op jit(solution)/shard_map/ppermute | solution.py:12
  15.4 1.1 maximum_select_fusion.5
  16.5 2.8 %collective-permute-start.1 = (bf16[32,5120]{1,0:T(8,128)(2,1)S(1)}, bf16[32,5120]{1,0:T(8,128)(2,1)S(1)}, u32[]{:S(2)}, u32[]{:S(2)}) collective-permute-start(bf16[32,5120]{1,0:T(8,128)(2,1)S(1)} %maximum_select_fusion.5), channel_id=1, source_target_pairs={{0,2},{1,3},{2,0},{3,1},{16,18},{17,19},{18,16},{19,17},{4,6},{5,7... | collective-permute-start | bytes 983048 | tf_op jit(solution)/shard_map/ppermute | solution.py:12
  19.3 14.0 %collective-permute-done.1 = bf16[32,5120]{1,0:T(8,128)(2,1)S(1)} collective-permute-done((bf16[32,5120]{1,0:T(8,128)(2,1)S(1)}, bf16[32,5120]{1,0:T(8,128)(2,1)S(1)}, u32[]{:S(2)}, u32[]{:S(2)}) %collective-permute-start.1) | collective-permute-done | bytes 327712 | tf_op jit(solution)/shard_map/ppermute | solution.py:12
  33.4 0.1 maximum_select_fusion.4
  33.5 0.1 collective-permute-start.2
  33.6 2.0 collective-permute-done.2
  35.6 81.9 %all-gather.2.cloned.1.call-done = bf16[5120,1024]{1,0:T(8,128)(2,1)} async-done(((bf16[1280,1024]{1,0:T(8,128)(2,1)}), bf16[5120,1024]{1,0:T(8,128)(2,1)}) %all-gather.2.cloned.1.call-update) | async-done | bytes 10485776 | tf_op jit(solution)/shard_map/all_gather | solution.py:29
  117.5 6.2 %fusion.16 = bf16[128,1024]{1,0:T(8,128)(2,1)} fusion(bf16[5120,1024]{1,0:T(8,128)(2,1)} %all-gather.2.cloned.1.call-done, bf16[64,5120]{1,0:T(8,128)(2,1)S(1)} %collective-permute-done.2, bf16[64,5120]{1,0:T(8,128)(2,1)S(1)} %maximum_select_fusion.4, pred[]{:T(512)S(6)} %eq.25), kind=kOutput, calls=%fused_computation.22 | convolution fusion | flops 1348206592 | bytes 12058625 | tf_op jit(solution)/shard_map/dot_general | solution.py:30
  123.7 4.7 %all-to-all-start = ((bf16[8,16,1024]{2,1,0:T(8,128)(2,1)}), bf16[8,16,1024]{2,1,0:T(8,128)(2,1)S(1)}, u32[]{:S(2)}, u32[]{:S(2)}) async-start(bf16[8,16,1024]{2,1,0:T(8,128)(2,1)} %bitcast), calls=%async_computation | async-start | bytes 524288 | tf_op jit(solution)/shard_map/all_to_all | solution.py:31
  128.5 0.6 reduce_sum.36
  129.2 0.7 add_compare_fusion
  129.8 0.1 fusion.20
  129.9 7.9 %all-to-all-done = bf16[8,16,1024]{2,1,0:T(8,128)(2,1)S(1)} async-done(((bf16[8,16,1024]{2,1,0:T(8,128)(2,1)}), bf16[8,16,1024]{2,1,0:T(8,128)(2,1)S(1)}, u32[]{:S(2)}, u32[]{:S(2)}) %all-to-all-start) | async-done | bytes 262176 | tf_op jit(solution)/shard_map/all_to_all | solution.py:31
  137.9 1.0 multiply_reduce_fusion
  138.9 0.6 copy-done.1
  139.4 1.5 fusion.7
  141.0 1.1 fusion
  142.1 11.8 %all_to_all.38 = bf16[16,8,1024]{2,0,1:T(8,128)(2,1)S(1)} all-to-all(bf16[16,8,1024]{2,0,1:T(8,128)(2,1)S(1)} %bitcast.20), channel_id=1, replica_groups=mesh['grp'=2,'dp'=4,'sp'=4] {'grp','sp'}, dimensions={1} | all-to-all | bytes 524288 | tf_op jit(solution)/shard_map/all_to_all | solution.py:52
  153.9 4.6 %convolution_convert_fusion = bf16[128,5120]{1,0:T(8,128)(2,1)} fusion(bf16[128,1024]{1,0:T(8,128)(2,1)S(1)} %bitcast.18, bf16[5120,1024]{1,0:T(8,128)(2,1)S(1)} %bitcast.16), kind=kOutput, calls=%fused_computation.3 | convolution fusion | flops 1342832640 | bytes 12058624 | tf_op jit(solution)/shard_map/dot_general | solution.py:53
  158.6 39.6 %psum.7 = f32[8192]{0:T(1024)} all-reduce(f32[8192]{0:T(1024)S(1)} %get-tuple-element.2), channel_id=1, replica_groups=mesh['grp'=2,'dp'=4,'sp'=4] {'grp','dp','sp'}, use_global_device_ids=true, to_apply=%region_6.7 | all-reduce | flops 8192 | bytes 65536 | tf_op jit(solution)/shard_map/psum | solution.py:59
  (23 shorter events, 0.1 us)
Async XLA Ops:
  7.2 110.3 %all-gather.2.cloned.1.call-start = ((), (), s32[]{:S(2)}) async-start(), calls=%async_computation.3 | async-start | bytes 13107200 | tf_op jit(solution)/shard_map/all_gather | solution.py:29
  7.9 7.5 %collective-permute-start = (bf16[16,5120]{1,0:T(8,128)(2,1)}, bf16[16,5120]{1,0:T(8,128)(2,1)S(1)}, u32[]{:S(2)}, u32[]{:S(2)}) collective-permute-start(bf16[16,5120]{1,0:T(8,128)(2,1)} %param.7), channel_id=1, source_target_pairs={{0,1},{1,0},{2,3},{3,2},{16,17},{17,16},{18,19},{19,18},{4,5},{5,4... | collective-permute-start | bytes 491528 | tf_op jit(solution)/shard_map/ppermute | solution.py:12
  16.5 16.9 %collective-permute-start.1 = (bf16[32,5120]{1,0:T(8,128)(2,1)S(1)}, bf16[32,5120]{1,0:T(8,128)(2,1)S(1)}, u32[]{:S(2)}, u32[]{:S(2)}) collective-permute-start(bf16[32,5120]{1,0:T(8,128)(2,1)S(1)} %maximum_select_fusion.5), channel_id=1, source_target_pairs={{0,2},{1,3},{2,0},{3,1},{16,18},{17,19},{18,16},{19,17},{4,6},{5,7... | collective-permute-start | bytes 983048 | tf_op jit(solution)/shard_map/ppermute | solution.py:12
  33.5 2.2 %collective-permute-start.2 = (bf16[64,5120]{1,0:T(8,128)(2,1)S(1)}, bf16[64,5120]{1,0:T(8,128)(2,1)S(1)}, u32[]{:S(2)}, u32[]{:S(2)}) collective-permute-start(bf16[64,5120]{1,0:T(8,128)(2,1)S(1)} %maximum_select_fusion.4), channel_id=1, source_target_pairs={{0,16},{1,17},{2,18},{3,19},{16,0},{17,1},{18,2},{19,3},{4,20},{5,... | collective-permute-start | bytes 1966088 | tf_op jit(solution)/shard_map/ppermute | solution.py:12
  33.5 95.0 %copy-start.4 = (s32[8]{0:T(128)S(1)}, s32[8]{0:T(128)}, u32[]{:S(2)}) copy-start(s32[8]{0:T(128)} %param.9) | copy-start | bytes 100
  33.6 96.3 %copy-start.3 = (s32[16]{0:T(128)S(1)}, s32[16]{0:T(128)}, u32[]{:S(2)}) copy-start(s32[16]{0:T(128)} %param.10) | copy-start | bytes 196
  33.6 104.3 %copy-start = (bf16[128,8192]{1,0:T(8,128)(2,1)S(1)}, bf16[128,8192]{1,0:T(8,128)(2,1)}, u32[]{:S(2)}) copy-start(bf16[128,8192]{1,0:T(8,128)(2,1)} %param.11) | copy-start | bytes 6291460
  123.7 15.1 %copy-start.2 = (f32[8192]{0:T(1024)S(1)}, f32[8192]{0:T(1024)}, u32[]{:S(2)}) copy-start(f32[8192]{0:T(1024)} %param.13) | copy-start | bytes 98308
  123.7 14.1 %all-to-all-start = ((bf16[8,16,1024]{2,1,0:T(8,128)(2,1)}), bf16[8,16,1024]{2,1,0:T(8,128)(2,1)S(1)}, u32[]{:S(2)}, u32[]{:S(2)}) async-start(bf16[8,16,1024]{2,1,0:T(8,128)(2,1)} %bitcast), calls=%async_computation | async-start | bytes 524288 | tf_op jit(solution)/shard_map/all_to_all | solution.py:31
  128.5 69.7 %reduce-scatter.2.cloned.1.call-start = ((), (), s32[]{:S(2)}) async-start(), calls=%async_computation.4 | async-start | bytes 1474560 | tf_op jit(solution)/shard_map/reduce_scatter | solution.py:56
  137.8 1.6 copy-start.1
  137.9 16.0 %slice-start = ((s8[10485760]{0:T(1024)(128)(4,1)}), s8[4194304]{0:T(1024)(128)(4,1)S(1)}, s32[]{:S(2)}) async-start(s8[10485760]{0:T(1024)(128)(4,1)} %bitcast.15), calls=%async_computation.5 | async-start | bytes 8388608
  139.4 14.5 %slice-start.1 = ((s8[10485760]{0:T(1024)(128)(4,1)}), s8[4194304]{0:T(1024)(128)(4,1)S(1)}, s32[]{:S(2)}) async-start(s8[10485760]{0:T(1024)(128)(4,1)} %bitcast.15), calls=%async_computation.6 | async-start | bytes 8388608
  140.9 13.0 %slice-start.2 = ((s8[10485760]{0:T(1024)(128)(4,1)}), s8[2097152]{0:T(1024)(128)(4,1)S(1)}, s32[]{:S(2)}) async-start(s8[10485760]{0:T(1024)(128)(4,1)} %bitcast.15), calls=%async_computation.7 | async-start | bytes 4194304
Sparse Core Ops, SparseCore 0:
  9.8 107.6 all-gather.1
  158.7 35.0 reduce-scatter.1
